TPU v7x, 32 devices: a whole 2x2x4 slice. The times are simulated.
32 devices in a mesh: dp: 8 (over z, x), fsdp: 4 (over y, core).
Axes of the slice: x: 2, y: 2, z: 4, core: 2. Of those that a mesh axis runs over, the one named last changes fastest.
Arguments:
- latents: float32 [96, 256, 384], P(('dp', 'fsdp')), may hold values from -6 to 6
- conditioning: float32 [96, 384], P(('dp', 'fsdp')), may hold values from -6 to 6
- seq_counts: int32 [32], P(('dp', 'fsdp')), may hold values from 1 to 3, as said below
- cotangent: float32 [96, 256, 384], P(('dp', 'fsdp')), may hold values from -6 to 6
- ada_weight: bfloat16 [2, 384, 2304], P(None, 'fsdp'), may hold values from -0.3125 to 0.3125
- ada_bias: bfloat16 [2, 2304], P(None, 'fsdp'), may hold values from -2.390625 to 2.390625
- qkv_weight: bfloat16 [2, 384, 1152], P(None, 'fsdp'), may hold values from -0.3125 to 0.3125
- proj_weight: bfloat16 [2, 384, 384], P(None, 'fsdp'), may hold values from -6 to 6
- proj_bias: bfloat16 [2, 384], P(None, 'fsdp'), may hold values from -3.59375 to 3.59375
- up_weight: bfloat16 [2, 384, 1536], P(None, 'fsdp'), may hold values from -0.3125 to 0.3125
- up_bias: bfloat16 [2, 1536], P(None, 'fsdp'), may hold values from -3.59375 to 3.59375
- down_weight: bfloat16 [2, 1536, 384], P(None, 'fsdp'), may hold values from -0.15625 to 0.15625
- down_bias: bfloat16 [2, 384], P(None, 'fsdp'), may hold values from -3.59375 to 3.59375
Outputs:
- block_out: float32 [96, 256, 384], P(('dp', 'fsdp'))
- grad_latents: float32 [96, 256, 384], P(('dp', 'fsdp'))
- grad_conditioning: float32 [96, 384], P(('dp', 'fsdp'))
- grad_ada_weight: float32 [2, 384, 2304], P(None, 'fsdp')
- grad_ada_bias: float32 [2, 2304], P(None, 'fsdp')
- grad_qkv_weight: float32 [2, 384, 1152], P(None, 'fsdp')
- grad_proj_weight: float32 [2, 384, 384], P(None, 'fsdp')
- grad_proj_bias: float32 [2, 384], P(None, 'fsdp')
- grad_up_weight: float32 [2, 384, 1536], P(None, 'fsdp')
- grad_up_bias: float32 [2, 1536], P(None, 'fsdp')
- grad_down_weight: float32 [2, 1536, 384], P(None, 'fsdp')
- grad_down_bias: float32 [2, 384], P(None, 'fsdp')
Inputs may be any that keep to these rules, and one draw needn't show every extreme that they name: `seq_counts`: number of live sequences of a device; its slots from that number on are padding.
All inputs are finite; a program needn't handle non-finite values.
Results may differ from a plain program's by a relative error of at most 0.014.
Values may be sent and summed in bfloat16 or wider, within the bound.
No kernel may reach another device: no remote copies, remote signals or barrier semaphores. Data moves between devices by JAX's collectives and lax.ppermute only.
A program may use at most 192 MiB of HBM per device.

v0:
```python
import jax
import jax.numpy as jnp
from jax import lax
from jax.sharding import PartitionSpec as P

HEADS = 6
LAYERS = 2
NORM_EPS = 1e-06
GELU_K = 0.7978845608028654
GELU_C = 0.044715


def einsum_mixed(form, left, right):
    return jnp.einsum(form, left, right, preferred_element_type=jnp.float32)


def matmul_last(left, right):
    flat = left.reshape(-1, left.shape[-1])
    return jnp.dot(flat, right, preferred_element_type=jnp.float32).reshape(
        left.shape[:-1] + (right.shape[1],)
    )


def matmul_back(left, right):
    flat = left.reshape(-1, left.shape[-1])
    return jnp.dot(flat, right.T, preferred_element_type=jnp.float32).reshape(
        left.shape[:-1] + (right.shape[0],)
    )


def outer_total(left, right):
    return jnp.dot(
        left.reshape(-1, left.shape[-1]).T,
        right.reshape(-1, right.shape[-1]),
        preferred_element_type=jnp.float32,
    )


def norm_rows(values):
    center = values - jnp.mean(values, axis=-1, keepdims=True)
    inv_std = lax.rsqrt(jnp.mean(center * center, axis=-1, keepdims=True) + NORM_EPS)
    return (center * inv_std, inv_std)


def norm_back(normed, inv_std, grad_normed):
    mean_grad = jnp.mean(grad_normed, axis=-1, keepdims=True)
    mean_prod = jnp.mean(grad_normed * normed, axis=-1, keepdims=True)
    return inv_std * (grad_normed - mean_grad - normed * mean_prod)


def gelu_tanh(values):
    inner = GELU_K * (values + GELU_C * values * values * values)
    return 0.5 * values * (1.0 + jnp.tanh(inner))


def gelu_slope(values):
    tangent = jnp.tanh(GELU_K * (values + GELU_C * values * values * values))
    return 0.5 * (1.0 + tangent) + 0.5 * values * (1.0 - tangent * tangent) * GELU_K * (
        1.0 + 3.0 * GELU_C * values * values
    )


def silu_slope(values):
    sigm = jax.nn.sigmoid(values)
    return sigm * (1.0 + values * (1.0 - sigm))


def split_heads(qkv):
    seq_slots, length, triple = qkv.shape
    width = triple // 3
    split = qkv.reshape(seq_slots, length, 3, HEADS, width // HEADS)
    return (split[:, :, 0], split[:, :, 1], split[:, :, 2])


def attend(qkv):
    queries, keys, values = split_heads(qkv)
    scale = 1.0 / jnp.sqrt(jnp.float32(queries.shape[-1]))
    scores = einsum_mixed("sqhd,skhd->shqk", queries, keys) * scale
    top = jnp.max(scores, axis=-1, keepdims=True)
    expo = jnp.exp(scores - top)
    probs = expo / jnp.sum(expo, axis=-1, keepdims=True)
    probs_low = probs.astype(jnp.bfloat16)
    mixed = einsum_mixed("shqk,skhd->sqhd", probs_low, values).astype(jnp.bfloat16)
    return (probs, probs_low, mixed.reshape(qkv.shape[0], qkv.shape[1], -1))


def attend_back(qkv, probs, probs_low, grad_mixed):
    queries, keys, values = split_heads(qkv)
    scale = 1.0 / jnp.sqrt(jnp.float32(queries.shape[-1]))
    grad_heads = grad_mixed.reshape(values.shape)
    grad_probs = einsum_mixed("sqhd,skhd->shqk", grad_heads, values)
    grad_values = einsum_mixed("shqk,sqhd->skhd", probs_low, grad_heads)
    row_dot = jnp.sum(probs * grad_probs, axis=-1, keepdims=True)
    grad_scores = (probs * (grad_probs - row_dot) * scale).astype(jnp.bfloat16)
    grad_queries = einsum_mixed("shqk,skhd->sqhd", grad_scores, keys)
    grad_keys = einsum_mixed("shqk,sqhd->skhd", grad_scores, queries)
    joined = jnp.stack([grad_queries, grad_keys, grad_values], axis=2)
    return joined.reshape(qkv.shape).astype(jnp.bfloat16)


def layer_parts(resid, cond, weights):
    (
        ada_weight,
        ada_bias,
        qkv_weight,
        proj_weight,
        proj_bias,
        up_weight,
        up_bias,
        down_weight,
        down_bias,
    ) = weights
    width = resid.shape[-1]
    act_low = jax.nn.silu(cond).astype(jnp.bfloat16)
    ada = jnp.dot(act_low, ada_weight, preferred_element_type=jnp.float32) + ada_bias.astype(
        jnp.float32
    )
    mods = [ada[:, None, piece_idx * width : (piece_idx + 1) * width] for piece_idx in range(6)]
    normed_one, inv_one = norm_rows(resid)
    attn_in = (normed_one * (1.0 + mods[1]) + mods[0]).astype(jnp.bfloat16)
    qkv = matmul_last(attn_in, qkv_weight).astype(jnp.bfloat16)
    probs, probs_low, mixed = attend(qkv)
    attn = matmul_last(mixed, proj_weight) + proj_bias.astype(jnp.float32)
    resid_one = resid + mods[2] * attn
    normed_two, inv_two = norm_rows(resid_one)
    mlp_in = (normed_two * (1.0 + mods[4]) + mods[3]).astype(jnp.bfloat16)
    pre_act = matmul_last(mlp_in, up_weight) + up_bias.astype(jnp.float32)
    hidden = gelu_tanh(pre_act).astype(jnp.bfloat16)
    branch = matmul_last(hidden, down_weight) + down_bias.astype(jnp.float32)
    result = resid_one + mods[5] * branch
    return dict(
        act_low=act_low,
        mods=mods,
        normed_one=normed_one,
        inv_one=inv_one,
        attn_in=attn_in,
        qkv=qkv,
        probs=probs,
        probs_low=probs_low,
        mixed=mixed,
        attn=attn,
        normed_two=normed_two,
        inv_two=inv_two,
        mlp_in=mlp_in,
        pre_act=pre_act,
        hidden=hidden,
        branch=branch,
        result=result,
    )


def layer_backward(resid, cond, weights, grad_out):
    (
        ada_weight,
        ada_bias,
        qkv_weight,
        proj_weight,
        proj_bias,
        up_weight,
        up_bias,
        down_weight,
        down_bias,
    ) = weights
    saved = layer_parts(resid, cond, weights)
    mods = saved["mods"]
    grad_gate_two = jnp.sum(grad_out * saved["branch"], axis=1)
    grad_branch = grad_out * mods[5]
    grad_down_bias = jnp.sum(grad_branch, axis=(0, 1))
    branch_low = grad_branch.astype(jnp.bfloat16)
    grad_down_weight = outer_total(saved["hidden"], branch_low)
    grad_pre = matmul_back(branch_low, down_weight) * gelu_slope(saved["pre_act"])
    grad_up_bias = jnp.sum(grad_pre, axis=(0, 1))
    pre_low = grad_pre.astype(jnp.bfloat16)
    grad_up_weight = outer_total(saved["mlp_in"], pre_low)
    grad_mlp = matmul_back(pre_low, up_weight)
    grad_shift_two = jnp.sum(grad_mlp, axis=1)
    grad_scale_two = jnp.sum(grad_mlp * saved["normed_two"], axis=1)
    grad_one = grad_out + norm_back(
        saved["normed_two"], saved["inv_two"], grad_mlp * (1.0 + mods[4])
    )
    grad_gate_one = jnp.sum(grad_one * saved["attn"], axis=1)
    grad_attn = grad_one * mods[2]
    grad_proj_bias = jnp.sum(grad_attn, axis=(0, 1))
    attn_low = grad_attn.astype(jnp.bfloat16)
    grad_proj_weight = outer_total(saved["mixed"], attn_low)
    grad_mixed = matmul_back(attn_low, proj_weight).astype(jnp.bfloat16)
    grad_qkv = attend_back(saved["qkv"], saved["probs"], saved["probs_low"], grad_mixed)
    grad_qkv_weight = outer_total(saved["attn_in"], grad_qkv)
    grad_in = matmul_back(grad_qkv, qkv_weight)
    grad_shift_one = jnp.sum(grad_in, axis=1)
    grad_scale_one = jnp.sum(grad_in * saved["normed_one"], axis=1)
    grad_resid = grad_one + norm_back(
        saved["normed_one"], saved["inv_one"], grad_in * (1.0 + mods[1])
    )
    grad_ada = jnp.concatenate(
        [
            grad_shift_one,
            grad_scale_one,
            grad_gate_one,
            grad_shift_two,
            grad_scale_two,
            grad_gate_two,
        ],
        axis=-1,
    )
    grad_ada_bias = jnp.sum(grad_ada, axis=0)
    ada_low = grad_ada.astype(jnp.bfloat16)
    grad_ada_weight = jnp.dot(saved["act_low"].T, ada_low, preferred_element_type=jnp.float32)
    grad_cond = jnp.dot(ada_low, ada_weight.T, preferred_element_type=jnp.float32) * silu_slope(
        cond
    )
    grads = (
        grad_ada_weight,
        grad_ada_bias,
        grad_qkv_weight,
        grad_proj_weight,
        grad_proj_bias,
        grad_up_weight,
        grad_up_bias,
        grad_down_weight,
        grad_down_bias,
    )
    return (grad_resid, grad_cond, grads)


def gather_forward(stacks, layer_idx):
    (
        ada_weight,
        ada_bias,
        qkv_weight,
        proj_weight,
        proj_bias,
        up_weight,
        up_bias,
        down_weight,
        down_bias,
    ) = stacks
    return (
        lax.all_gather(ada_weight[layer_idx], "fsdp", axis=0, tiled=True),
        lax.all_gather(ada_bias[layer_idx], "fsdp", axis=0, tiled=True),
        lax.all_gather(qkv_weight[layer_idx], "fsdp", axis=0, tiled=True),
        lax.all_gather(proj_weight[layer_idx], "fsdp", axis=0, tiled=True),
        lax.all_gather(proj_bias[layer_idx], "fsdp", axis=0, tiled=True),
        lax.all_gather(up_weight[layer_idx], "fsdp", axis=0, tiled=True),
        lax.all_gather(up_bias[layer_idx], "fsdp", axis=0, tiled=True),
        lax.all_gather(down_weight[layer_idx], "fsdp", axis=0, tiled=True),
        lax.all_gather(down_bias[layer_idx], "fsdp", axis=0, tiled=True),
    )


def gather_backward(stacks, layer_idx):
    (
        ada_weight,
        ada_bias,
        qkv_weight,
        proj_weight,
        proj_bias,
        up_weight,
        up_bias,
        down_weight,
        down_bias,
    ) = stacks
    return (
        lax.all_gather(ada_weight[layer_idx], "fsdp", axis=0, tiled=True),
        lax.all_gather(ada_bias[layer_idx], "fsdp", axis=0, tiled=True),
        lax.all_gather(qkv_weight[layer_idx], "fsdp", axis=0, tiled=True),
        lax.all_gather(proj_weight[layer_idx], "fsdp", axis=0, tiled=True),
        lax.all_gather(proj_bias[layer_idx], "fsdp", axis=0, tiled=True),
        lax.all_gather(up_weight[layer_idx], "fsdp", axis=0, tiled=True),
        lax.all_gather(up_bias[layer_idx], "fsdp", axis=0, tiled=True),
        lax.all_gather(down_weight[layer_idx], "fsdp", axis=0, tiled=True),
        lax.all_gather(down_bias[layer_idx], "fsdp", axis=0, tiled=True),
    )


def reduce_layer(grads):
    shards = (
        lax.psum_scatter(grads[0], "fsdp", scatter_dimension=0, tiled=True),
        lax.psum_scatter(grads[1], "fsdp", scatter_dimension=0, tiled=True),
        lax.psum_scatter(grads[2], "fsdp", scatter_dimension=0, tiled=True),
        lax.psum_scatter(grads[3], "fsdp", scatter_dimension=0, tiled=True),
        lax.psum_scatter(grads[4], "fsdp", scatter_dimension=0, tiled=True),
        lax.psum_scatter(grads[5], "fsdp", scatter_dimension=0, tiled=True),
        lax.psum_scatter(grads[6], "fsdp", scatter_dimension=0, tiled=True),
        lax.psum_scatter(grads[7], "fsdp", scatter_dimension=0, tiled=True),
        lax.psum_scatter(grads[8], "fsdp", scatter_dimension=0, tiled=True),
    )
    return lax.psum(
        (
            shards[0],
            shards[1],
            shards[2],
            shards[3],
            shards[4],
            shards[5],
            shards[6],
            shards[7],
            shards[8],
        ),
        "dp",
    )


def on_device(
    latents,
    conditioning,
    seq_counts,
    cotangent,
    ada_weight,
    ada_bias,
    qkv_weight,
    proj_weight,
    proj_bias,
    up_weight,
    up_bias,
    down_weight,
    down_bias,
):
    stacks = (
        ada_weight,
        ada_bias,
        qkv_weight,
        proj_weight,
        proj_bias,
        up_weight,
        up_bias,
        down_weight,
        down_bias,
    )
    seq_slots = latents.shape[0]
    live = (jnp.arange(seq_slots, dtype=jnp.int32) < seq_counts[0]).astype(jnp.float32)[
        :, None, None
    ]
    inputs = []
    gathered = []
    current = latents
    for layer_idx in range(LAYERS):
        weights = gather_forward(stacks, layer_idx)
        gathered.append(weights)
        inputs.append(current)
        current = layer_parts(current, conditioning, weights)["result"]
    block_out = current * live
    grad = cotangent * live
    grad_cond = jnp.zeros(conditioning.shape, jnp.float32)
    layer_grads = [None] * LAYERS
    for layer_idx in reversed(range(LAYERS)):
        weights = gather_backward(stacks, layer_idx)
        grad, cond_part, grads = layer_backward(inputs[layer_idx], conditioning, weights, grad)
        grad_cond = grad_cond + cond_part
        layer_grads[layer_idx] = reduce_layer(grads)
    finals = [
        jnp.stack([layer_grads[layer_idx][piece_idx] for layer_idx in range(LAYERS)], axis=0)
        for piece_idx in range(9)
    ]
    return (
        block_out,
        grad,
        grad_cond,
        finals[0],
        finals[1],
        finals[2],
        finals[3],
        finals[4],
        finals[5],
        finals[6],
        finals[7],
        finals[8],
    )


def solution(mesh):
    in_specs = (
        P(("dp", "fsdp"), None, None),
        P(("dp", "fsdp"), None),
        P(("dp", "fsdp")),
        P(("dp", "fsdp"), None, None),
        P(None, "fsdp", None),
        P(None, "fsdp"),
        P(None, "fsdp", None),
        P(None, "fsdp", None),
        P(None, "fsdp"),
        P(None, "fsdp", None),
        P(None, "fsdp"),
        P(None, "fsdp", None),
        P(None, "fsdp"),
    )
    out_specs = (
        P(("dp", "fsdp"), None, None),
        P(("dp", "fsdp"), None, None),
        P(("dp", "fsdp"), None),
        P(None, "fsdp", None),
        P(None, "fsdp"),
        P(None, "fsdp", None),
        P(None, "fsdp", None),
        P(None, "fsdp"),
        P(None, "fsdp", None),
        P(None, "fsdp"),
        P(None, "fsdp", None),
        P(None, "fsdp"),
    )
    return jax.shard_map(
        on_device, mesh=mesh, in_specs=in_specs, out_specs=out_specs, check_vma=False
    )
```

profile of v0, /device:TPU:0, one launch (start us, length us, event | category | flops | bytes accessed | tf_op | source)
XLA Modules:
  0.0 733.3 jit_solution(9864900961176631379)
XLA Ops:
  17.1 6.2 all-gather.15
  23.9 5.7 all-gather.6
  31.0 11.7 %all-reduce.17 = (bf16[2304]{0:T(1024)(128)(2,1)S(1)}, bf16[384]{0:T(512)(128)(2,1)S(1)}, bf16[384]{0:T(512)(128)(2,1)S(1)}, bf16[2304]{0:T(1024)(128)(2,1)S(1)}...) all-reduce(bf16[2304]{0:T(1024)(128)(2,1)S(1)} %dynamic-update-slice, ...), channel_id=3, replica_groups=mesh['dp'=8,'fsdp'=4] {'fsdp'}, use_global_device_ids=true, to_apply=%add | all-reduce | flops 6144 | bytes 24576
  43.9 8.0 %all-gather.12 = bf16[1,384,384]{2,1,0:T(8,128)(2,1)} all-gather(bf16[1,96,384]{2,1,0:T(8,128)(2,1)S(1)} %get-tuple-element.91), channel_id=14, replica_groups=mesh['dp'=8,'fsdp'=4] {'fsdp'}, dimensions={1}, use_global_device_ids=true | all-gather | bytes 368640 | tf_op jit(solution)/shard_map/all_gather | solution.py:242
  51.9 7.2 all-gather.3
  59.1 9.7 %all-gather.11 = bf16[1,384,1152]{2,1,0:T(8,128)(2,1)} all-gather(bf16[1,96,1152]{2,1,0:T(8,128)(2,1)S(1)} %get-tuple-element.89), channel_id=13, replica_groups=mesh['dp'=8,'fsdp'=4] {'fsdp'}, dimensions={1}, use_global_device_ids=true | all-gather | bytes 1105920 | tf_op jit(solution)/shard_map/all_gather | solution.py:241
  68.8 13.9 %all-gather.2 = bf16[1,384,1152]{2,1,0:T(8,128)(2,1)S(1)} all-gather(bf16[1,96,1152]{2,1,0:T(8,128)(2,1)S(1)} %get-tuple-element.90), channel_id=4, replica_groups=mesh['dp'=8,'fsdp'=4] {'fsdp'}, dimensions={1}, use_global_device_ids=true | all-gather | bytes 1105920 | tf_op jit(solution)/shard_map/all_gather | solution.py:241
  101.3 4.8 fusion.88
  106.1 5.7 fusion.135
  131.4 5.0 fusion.82
  136.4 4.6 all-gather.35.cloned.1.call-done
  141.0 7.6 %fusion.148 = (f32[1536]{0:T(1024)}, bf16[3,256,1536]{2,1,0:T(8,128)(2,1)S(1)}) fusion(f32[3,256,1536]{2,1,0:T(8,128)} %fusion.82, f32[1536]{0:T(1024)} %convert_reduce_fusion, bf16[1,1536,384]{2,1,0:T(8,128)(2,1)} %all-gather.35.cloned.1.call-done, f32[3,256,384]{2,1,0:T(8,128)} %param.16, f32[3]{0:T(128)} %compare_convert_fusion, ...), kind=kOutput, calls=%fused_computation.256 | convolution fusion | flops 931625472 | bytes 9454092 | tf_op jit(solution)/shard_map/dot_general | solution.py:26
  152.6 4.5 multiply_reduce_fusion.23
  170.8 9.1 %fusion.67 = bf16[3,256,1,6,64]{1,4,3,0,2:T(8,128)(2,1)} fusion(f32[3,6,256,256]{2,3,1,0:T(8,128)} %fusion.112, bf16[3,256,3,6,64]{1,4,3,2,0:T(8,128)(2,1)} %bitcast.237, f32[3,6,256,256]{2,3,1,0:T(8,128)} %copy-done.18, f32[3,6,256]{2,1,0:T(8,128)} %copy-done.81), kind=kOutput, calls=%fused_computation.80 | convolution fusion | flops 159552256 | bytes 20103168 | tf_op jit(solution)/shard_map/shqk,skhd->sqhd/dot_general | solution.py:14
  179.8 8.9 %fusion.64 = bf16[3,256,1,6,64]{1,4,3,0,2:T(8,128)(2,1)} fusion(f32[3,6,256,256]{2,3,1,0:T(8,128)} %fusion.112, bf16[3,256,3,6,64]{1,4,3,2,0:T(8,128)(2,1)} %bitcast.238, f32[3,6,256,256]{2,3,1,0:T(8,128)} %copy-done.18, f32[3,6,256]{2,1,0:T(8,128)} %copy-done.81), kind=kOutput, calls=%fused_computation.79 | convolution fusion | flops 159552256 | bytes 20103168 | tf_op jit(solution)/shard_map/shqk,sqhd->skhd/dot_general | solution.py:14
  198.9 5.1 fusion.149
  225.4 9.0 %fusion.73 = bf16[3,256,1,6,64]{1,4,3,0,2:T(8,128)(2,1)} fusion(f32[3,6,256,256]{2,3,1,0:T(8,128)} %fusion.110, bf16[3,256,3,6,64]{1,4,3,2,0:T(8,128)(2,1)} %bitcast.232, f32[3,6,256,256]{2,3,1,0:T(8,128)} %copy-done.17, f32[3,6,256]{2,1,0:T(8,128)} %copy-done.80), kind=kOutput, calls=%fused_computation.82 | convolution fusion | flops 159552256 | bytes 20103168 | tf_op jit(solution)/shard_map/shqk,skhd->sqhd/dot_general | solution.py:14
  234.4 9.0 %fusion.70 = bf16[3,256,1,6,64]{1,4,3,0,2:T(8,128)(2,1)} fusion(f32[3,6,256,256]{2,3,1,0:T(8,128)} %fusion.110, bf16[3,256,3,6,64]{1,4,3,2,0:T(8,128)(2,1)} %bitcast.233, f32[3,6,256,256]{2,3,1,0:T(8,128)} %copy-done.17, f32[3,6,256]{2,1,0:T(8,128)} %copy-done.80), kind=kOutput, calls=%fused_computation.81 | convolution fusion | flops 159552256 | bytes 20103168 | tf_op jit(solution)/shard_map/shqk,sqhd->skhd/dot_general | solution.py:14
  251.1 6.5 convolution_bitcast_fusion
  257.7 4.4 convolution_bitcast_fusion.2
  263.3 6.3 convolution_bitcast_fusion.1
  270.4 4.4 convolution_bitcast_fusion.3
  286.0 16.1 %reduce-scatter.15.cloned.1.call-done = f32[96,1152]{1,0:T(8,128)} async-done(((f32[384,1152]{1,0:T(8,128)}), f32[96,1152]{1,0:T(8,128)}) %reduce-scatter.15.cloned.1.call-update) | async-done | bytes 442384 | tf_op jit(solution)/shard_map/reduce_scatter | solution.py:280
  302.0 35.4 %reduce-scatter.29.cloned.1.call-done = f32[384,384]{1,0:T(8,128)} async-done(((f32[1536,384]{1,0:T(8,128)}), f32[384,384]{1,0:T(8,128)}) %reduce-scatter.29.cloned.1.call-update) | async-done | bytes 589840 | tf_op jit(solution)/shard_map/reduce_scatter | solution.py:285
  337.4 35.2 %reduce-scatter.25.cloned.1.call-done = f32[96,1536]{1,0:T(8,128)} async-done(((f32[384,1536]{1,0:T(8,128)}), f32[96,1536]{1,0:T(8,128)}) %reduce-scatter.25.cloned.1.call-update) | async-done | bytes 589840 | tf_op jit(solution)/shard_map/reduce_scatter | solution.py:283
  372.6 35.4 %reduce-scatter.27.cloned.1.call-done = f32[384,384]{1,0:T(8,128)} async-done(((f32[1536,384]{1,0:T(8,128)}), f32[384,384]{1,0:T(8,128)}) %reduce-scatter.27.cloned.1.call-update) | async-done | bytes 589840 | tf_op jit(solution)/shard_map/reduce_scatter | solution.py:285
  408.0 35.2 %reduce-scatter.23.cloned.1.call-done = f32[96,1536]{1,0:T(8,128)} async-done(((f32[384,1536]{1,0:T(8,128)}), f32[96,1536]{1,0:T(8,128)}) %reduce-scatter.23.cloned.1.call-update) | async-done | bytes 589840 | tf_op jit(solution)/shard_map/reduce_scatter | solution.py:283
  443.3 42.8 %reduce-scatter.13.cloned.1.call-done = f32[96,2304]{1,0:T(8,128)} async-done(((f32[384,2304]{1,0:T(8,128)}), f32[96,2304]{1,0:T(8,128)}) %reduce-scatter.13.cloned.1.call-update) | async-done | bytes 884752 | tf_op jit(solution)/shard_map/reduce_scatter | solution.py:278
  486.1 42.8 %reduce-scatter.11.cloned.1.call-done = f32[96,2304]{1,0:T(8,128)} async-done(((f32[384,2304]{1,0:T(8,128)}), f32[96,2304]{1,0:T(8,128)}) %reduce-scatter.11.cloned.1.call-update) | async-done | bytes 884752 | tf_op jit(solution)/shard_map/reduce_scatter | solution.py:278
  531.2 10.6 %all-reduce.16 = (f32[2304]{0:T(1024)S(1)}, f32[2304]{0:T(1024)S(1)}, f32[384]{0:T(512)S(1)}, f32[384]{0:T(512)S(1)}, f32[1536]{0:T(1024)S(1)}, /*index=5*/f32[1536]{0:T(1024)S(1)}, f32[384]{0:T(512)S(1)}, f32[384]{0:T(512)S(1)}) all-reduce(f32[2304]{0:T(1024)S(1)} %reduce_sum.433, ...), channel_id=23, replica_groups=mesh['dp'=8,'fsdp'=4] {'fsdp'}, use_global_device_ids=true, to_apply=%region_42.43.clone | all-reduce | flops 9216 | bytes 73728
  542.4 39.5 %all-reduce.14 = (f32[1,576]{1,0:T(1,128)S(1)}, f32[1,576]{1,0:T(1,128)S(1)}, f32[1,96]{1,0:T(1,128)S(1)}, f32[1,96]{1,0:T(1,128)S(1)}, f32[1,384]{1,0:T(1,128)S...) all-reduce(f32[1,576]{1,0:T(1,128)S(1)} %stack.125, ...), channel_id=1, replica_groups=mesh['dp'=8,'fsdp'=4] {'dp'}, use_global_device_ids=true, to_apply=%region_43.44 | all-reduce | flops 2304 | bytes 18432 | tf_op jit(solution)/shard_map/psum | solution.py:288
  590.4 129.4 %all-reduce.20.cloned.1.call-done = (f32[1,96,2304]{2,1,0:T(8,128)}, f32[1,96,2304]{2,1,0:T(8,128)}, f32[1,96,1152]{2,1,0:T(8,128)}, f32[1,96,1152]{2,1,0:T(8,12...) async-done(((f32[1,96,2304]{2,1,0:T(8,128)}, ...) | async-done | bytes 5308432 | tf_op jit(solution)/shard_map/psum | solution.py:288
  (420 shorter events, 134.3 us)
Async XLA Ops:
  7.2 75.5 %all-gather.25.cloned.1.call-start = ((), (), s32[]{:S(2)}) async-start(), calls=%async_computation.20 | async-start | bytes 2211840 | tf_op jit(solution)/shard_map/all_gather | solution.py:239
  9.5 75.5 %all-gather.31.cloned.1.call-start = ((), (), s32[]{:S(2)}) async-start(), calls=%async_computation.23 | async-start | bytes 2211840 | tf_op jit(solution)/shard_map/all_gather | solution.py:239
  10.3 91.0 %all-gather.27.cloned.1.call-start = ((), (), s32[]{:S(2)}) async-start(), calls=%async_computation.21 | async-start | bytes 1474560 | tf_op jit(solution)/shard_map/all_gather | solution.py:244
  11.2 94.9 %all-gather.29.cloned.1.call-start = ((), (), s32[]{:S(2)}) async-start(), calls=%async_computation.22 | async-start | bytes 1474560 | tf_op jit(solution)/shard_map/all_gather | solution.py:246
  12.1 31.7 %copy-start.52 = (bf16[2,96,384]{2,1,0:T(8,128)(2,1)S(1)}, bf16[2,96,384]{2,1,0:T(8,128)(2,1)}, u32[]{:S(2)}) copy-start(bf16[2,96,384]{2,1,0:T(8,128)(2,1)} %param.20) | copy-start | bytes 442372
  12.2 119.2 %all-gather.33.cloned.1.call-start = ((), (), s32[]{:S(2)}) async-start(), calls=%async_computation.24 | async-start | bytes 1474560 | tf_op jit(solution)/shard_map/all_gather | solution.py:244
  12.8 128.2 %all-gather.35.cloned.1.call-start = ((), (), s32[]{:S(2)}) async-start(), calls=%async_computation.25 | async-start | bytes 1474560 | tf_op jit(solution)/shard_map/all_gather | solution.py:246
  13.3 272.6 %reduce-scatter.21.cloned.1.call-start = ((), (), s32[]{:S(2)}) async-start(), calls=%async_computation.15 | async-start | bytes 737280 | tf_op jit(solution)/shard_map/reduce_scatter | solution.py:281
  16.5 42.6 %copy-start.48 = (bf16[2,96,1152]{2,1,0:T(8,128)(2,1)S(1)}, bf16[2,96,1152]{2,1,0:T(8,128)(2,1)}, u32[]{:S(2)}) copy-start(bf16[2,96,1152]{2,1,0:T(8,128)(2,1)} %param.19) | copy-start | bytes 1327108
  16.7 70.7 %copy-start.66 = (f32[3,256]{1,0:T(4,128)}, f32[3,256]{1,0:T(4,128)S(1)}, u32[]{:S(2)}) copy-start(f32[3,256]{1,0:T(4,128)S(1)} %broadcast_multiply_fusion.11) | copy-start | bytes 9220
  17.1 70.4 %copy-start.82 = (f32[3,256]{1,0:T(4,128)}, f32[3,256]{1,0:T(4,128)S(1)}, u32[]{:S(2)}) copy-start(f32[3,256]{1,0:T(4,128)S(1)} %add_rsqrt_fusion.3) | copy-start | bytes 9220
  29.6 76.5 %copy-start.91 = (f32[1536]{0:T(1024)}, f32[1536]{0:T(1024)S(1)}, u32[]{:S(2)}) copy-start(f32[1536]{0:T(1024)S(1)} %convert_reduce_fusion.1) | copy-start | bytes 18436
  51.9 30.9 %copy-start.49 = (f32[3,384]{1,0:T(4,128)S(1)}, f32[3,384]{1,0:T(4,128)}, u32[]{:S(2)}) copy-start(f32[3,384]{1,0:T(4,128)} %param.14) | copy-start | bytes 13828
  59.1 40.1 %copy-start.19 = (bf16[1,384,384]{2,1,0:T(8,128)(2,1)}, bf16[1,384,384]{2,1,0:T(8,128)(2,1)S(1)}, u32[]{:S(2)}) copy-start(bf16[1,384,384]{2,1,0:T(8,128)(2,1)S(1)} %all-gather.3) | copy-start | bytes 884740
  84.9 14.3 %copy-start.59 = (f32[3,384]{1,0:T(4,128)}, f32[3,384]{1,0:T(4,128)S(1)}, u32[]{:S(2)}) copy-start(f32[3,384]{1,0:T(4,128)S(1)} %get-tuple-element.104) | copy-start | bytes 13828
  84.9 16.3 %copy-start.56 = (f32[3,384]{1,0:T(4,128)}, f32[3,384]{1,0:T(4,128)S(1)}, u32[]{:S(2)}) copy-start(f32[3,384]{1,0:T(4,128)S(1)} %get-tuple-element.101) | copy-start | bytes 13828
  84.9 16.3 %copy-start.61 = (f32[3,384]{1,0:T(4,128)}, f32[3,384]{1,0:T(4,128)S(1)}, u32[]{:S(2)}) copy-start(f32[3,384]{1,0:T(4,128)S(1)} %get-tuple-element.100) | copy-start | bytes 13828
  84.9 21.2 %copy-start.74 = (f32[3,384]{1,0:T(4,128)}, f32[3,384]{1,0:T(4,128)S(1)}, u32[]{:S(2)}) copy-start(f32[3,384]{1,0:T(4,128)S(1)} %get-tuple-element.99) | copy-start | bytes 13828
  87.4 24.8 %copy-start.76 = (f32[3,384]{1,0:T(4,128)}, f32[3,384]{1,0:T(4,128)S(1)}, u32[]{:S(2)}) copy-start(f32[3,384]{1,0:T(4,128)S(1)} %get-tuple-element.97) | copy-start | bytes 13828
  87.4 24.8 %copy-start.99 = (f32[3,384]{1,0:T(4,128)}, f32[3,384]{1,0:T(4,128)S(1)}, u32[]{:S(2)}) copy-start(f32[3,384]{1,0:T(4,128)S(1)} %get-tuple-element.96) | copy-start | bytes 13828
  141.0 9.9 %copy-start.117 = (bf16[1,1536,384]{2,1,0:T(8,128)(2,1)S(1)}, bf16[1,1536,384]{2,1,0:T(8,128)(2,1)}, u32[]{:S(2)}) copy-start(bf16[1,1536,384]{2,1,0:T(8,128)(2,1)} %all-gather.35.cloned.1.call-done) | copy-start | bytes 3538948
  191.9 94.1 %reduce-scatter.19.cloned.1.call-start = ((), (), s32[]{:S(2)}) async-start(), calls=%async_computation.14 | async-start | bytes 737280 | tf_op jit(solution)/shard_map/reduce_scatter | solution.py:281
  211.9 74.0 %reduce-scatter.17.cloned.1.call-start = ((), (), s32[]{:S(2)}) async-start(), calls=%async_computation.13 | async-start | bytes 2211840 | tf_op jit(solution)/shard_map/reduce_scatter | solution.py:280
  216.4 85.7 %reduce-scatter.15.cloned.1.call-start = ((), (), s32[]{:S(2)}) async-start(), calls=%async_computation.12 | async-start | bytes 2211840 | tf_op jit(solution)/shard_map/reduce_scatter | solution.py:280
  251.1 86.3 %reduce-scatter.29.cloned.1.call-start = ((), (), s32[]{:S(2)}) async-start(), calls=%async_computation.19 | async-start | bytes 2949120 | tf_op jit(solution)/shard_map/reduce_scatter | solution.py:285
  257.6 115.0 %reduce-scatter.25.cloned.1.call-start = ((), (), s32[]{:S(2)}) async-start(), calls=%async_computation.17 | async-start | bytes 2949120 | tf_op jit(solution)/shard_map/reduce_scatter | solution.py:283
  262.1 145.9 %reduce-scatter.27.cloned.1.call-start = ((), (), s32[]{:S(2)}) async-start(), calls=%async_computation.18 | async-start | bytes 2949120 | tf_op jit(solution)/shard_map/reduce_scatter | solution.py:285
  269.7 173.6 %reduce-scatter.23.cloned.1.call-start = ((), (), s32[]{:S(2)}) async-start(), calls=%async_computation.16 | async-start | bytes 2949120 | tf_op jit(solution)/shard_map/reduce_scatter | solution.py:283
  274.8 211.3 %reduce-scatter.13.cloned.1.call-start = ((), (), s32[]{:S(2)}) async-start(), calls=%async_computation.11 | async-start | bytes 4423680 | tf_op jit(solution)/shard_map/reduce_scatter | solution.py:278
  278.0 250.9 %reduce-scatter.11.cloned.1.call-start = ((), (), s32[]{:S(2)}) async-start(), calls=%async_computation.10 | async-start | bytes 4423680 | tf_op jit(solution)/shard_map/reduce_scatter | solution.py:278
  285.9 434.0 %all-reduce.20.cloned.1.call-start = ((), (), s32[]{:S(2)}) async-start(), calls=%async_computation.26 | async-start | bytes 10616832 | tf_op jit(solution)/shard_map/psum | solution.py:288
  529.0 57.4 %copy-start.7 = (bf16[1,384,2304]{2,1,0:T(8,128)(2,1)S(1)}, bf16[1,384,2304]{2,1,0:T(8,128)(2,1)}, u32[]{:S(2)}) copy-start(bf16[1,384,2304]{2,1,0:T(8,128)(2,1)} %all-gather.25.cloned.1.call-done) | copy-start | bytes 5308420
  (106 other events, 315.2 us)
Sparse Core Ops, SparseCore 0:
  10.1 23.4 all-gather.24
  35.8 23.4 all-gather.30
  61.5 21.6 all-gather.26
  85.1 17.4 all-gather.28
  104.0 17.4 all-gather.32
  123.5 17.4 all-gather.34
  192.0 22.0 reduce-scatter.20
  216.5 22.0 reduce-scatter.18
  241.2 29.1 reduce-scatter.16
  272.8 29.1 reduce-scatter.14
  304.6 32.7 reduce-scatter.28
  339.8 32.8 reduce-scatter.24
  375.2 32.8 reduce-scatter.26
  410.4 32.8 reduce-scatter.22
  445.7 40.3 reduce-scatter.12
  488.5 40.3 reduce-scatter.10
  533.5 186.2 all-reduce.19
where the time goes:
time: 738 us; the launch traced here: 733 us
  waiting for transfers between devices  379 us (51%)
  matrix products  156 us (21%)
  blocking collectives  112 us (15%)
  local copies, waits for them, and re-layouts  36.4 us (5%)
  other arithmetic  29 us (4%)
  between operations  19.4 us (3%)
    psum x1, waiting for transfers between devices, reduce_layer(): lax.psum((shards[0], shards[1], shards[2], shards[3], shards[4], shards[5...  129 us
    reduce_scatter x2, waiting for transfers between devices, reduce_layer(): lax.psum_scatter(grads[0], 'fsdp', scatter_dimension=0, tiled=True)  85.7 us
    reduce_scatter x2, waiting for transfers between devices, reduce_layer(): lax.psum_scatter(grads[7], 'fsdp', scatter_dimension=0, tiled=True)  70.7 us
    reduce_scatter x2, waiting for transfers between devices, reduce_layer(): lax.psum_scatter(grads[5], 'fsdp', scatter_dimension=0, tiled=True)  70.5 us
    dot_general x12, matrix products, einsum_mixed(): return jnp.einsum(form, left, right, preferred_element_type=jnp.float32)  57.6 us
    psum x1, blocking collectives, reduce_layer(): lax.psum((shards[0], shards[1], shards[2], shards[3], shards[4], shards[5...  39.5 us
    dot_general x8, matrix products, outer_total(): jnp.dot(left.reshape(-1, left.shape[-1]).T, right.reshape(-1, right.shape...  31.1 us
    dot_general x8, matrix products, matmul_last(): jnp.dot(flat, right, preferred_element_type=jnp.float32)  28.3 us
  transfers between devices with their start and end apart: 17, of which 9 were waited for; matrix products, arithmetic and copies ran while one was open for 20% of the time, Pallas kernels for 0%

commit v1 on v0

--- a/solution.py
+++ b/solution.py
@@ -8,6 +8,27 @@
 NORM_EPS = 1e-06
 GELU_K = 0.7978845608028654
 GELU_C = 0.044715
+
+
+def gather_around(value, axis, dim):
+    size, index, rows = (lax.axis_size(axis), lax.axis_index(axis), value.shape[dim])
+    right = [(i, (i + 1) % size) for i in range(size)]
+    left = [(i, (i - 1) % size) for i in range(size)]
+    result = jnp.zeros((*value.shape[:dim], size * rows, *value.shape[dim + 1 :]), value.dtype)
+    result = lax.dynamic_update_slice_in_dim(result, value, index * rows, axis=dim)
+    from_left = from_right = value
+    half = size // 2
+    for step in range(1, half + 1):
+        from_left = lax.ppermute(from_left, axis, right)
+        result = lax.dynamic_update_slice_in_dim(
+            result, from_left, (index - step) % size * rows, axis=dim
+        )
+        if step < size - half:
+            from_right = lax.ppermute(from_right, axis, left)
+            result = lax.dynamic_update_slice_in_dim(
+                result, from_right, (index + step) % size * rows, axis=dim
+            )
+    return result
 
 
 def einsum_mixed(form, left, right):
@@ -239,7 +260,7 @@
         lax.all_gather(ada_weight[layer_idx], "fsdp", axis=0, tiled=True),
         lax.all_gather(ada_bias[layer_idx], "fsdp", axis=0, tiled=True),
         lax.all_gather(qkv_weight[layer_idx], "fsdp", axis=0, tiled=True),
-        lax.all_gather(proj_weight[layer_idx], "fsdp", axis=0, tiled=True),
+        gather_around(proj_weight[layer_idx], "fsdp", 0),
         lax.all_gather(proj_bias[layer_idx], "fsdp", axis=0, tiled=True),
         lax.all_gather(up_weight[layer_idx], "fsdp", axis=0, tiled=True),
         lax.all_gather(up_bias[layer_idx], "fsdp", axis=0, tiled=True),

time: 738 us -> 733 us (level)
  waiting for transfers between devices: 379 us -> 355 us
    reduce_scatter x2, waiting for transfers between devices: 16.1 us -> 0.13 us  [reduce_layer(): lax.psum_scatter(grads[2], 'fsdp', scatter_dimension=0, tiled=True)]
    psum x1, waiting for transfers between devices: 129 us -> 117 us  [reduce_layer(): lax.psum((shards[0], shards[1], shards[2], shards[3], shards[4], shards[5...]
    dot_general x8 -> x12, matrix products: 28.3 us -> 37.6 us  [matmul_last(): jnp.dot(flat, right, preferred_element_type=jnp.float32)]
    unnamed x273 -> x295, local copies, waits for them, and re-layouts: 18.8 us -> 21.2 us
  transfers between devices with their start and end apart: 17 -> 23, of which waited for: 9 -> 12; matrix products, arithmetic and copies ran while one was open for 20% -> 23% of each run, Pallas kernels for 0% -> 0%
where the time goes in v1:
time: 733 us; the launch traced here: 726 us
  waiting for transfers between devices  355 us (48%)
  matrix products  162 us (22%)
  blocking collectives  112 us (15%)
  local copies, waits for them, and re-layouts  38.7 us (5%)
  other arithmetic  33.3 us (5%)
  between operations  19.5 us (3%)
    psum x1, waiting for transfers between devices, reduce_layer(): lax.psum((shards[0], shards[1], shards[2], shards[3], shards[4], shards[5...  117 us
    reduce_scatter x2, waiting for transfers between devices, reduce_layer(): lax.psum_scatter(grads[0], 'fsdp', scatter_dimension=0, tiled=True)  85.6 us
    reduce_scatter x2, waiting for transfers between devices, reduce_layer(): lax.psum_scatter(grads[7], 'fsdp', scatter_dimension=0, tiled=True)  70.8 us
    reduce_scatter x2, waiting for transfers between devices, reduce_layer(): lax.psum_scatter(grads[5], 'fsdp', scatter_dimension=0, tiled=True)  70.5 us
    dot_general x12, matrix products, einsum_mixed(): return jnp.einsum(form, left, right, preferred_element_type=jnp.float32)  57.9 us
    psum x1, blocking collectives, reduce_layer(): lax.psum((shards[0], shards[1], shards[2], shards[3], shards[4], shards[5...  40 us
    dot_general x12, matrix products, matmul_last(): jnp.dot(flat, right, preferred_element_type=jnp.float32)  37.6 us
    dot_general x8, matrix products, outer_total(): jnp.dot(left.reshape(-1, left.shape[-1]).T, right.reshape(-1, right.shape...  31 us
  transfers between devices with their start and end apart: 23, of which 12 were waited for; matrix products, arithmetic and copies ran while one was open for 23% of the time, Pallas kernels for 0%

profile of v1, /device:TPU:0, one launch (start us, length us, event | category | flops | bytes accessed | tf_op | source)
XLA Modules:
  0.0 726.4 jit_solution(9228827964230624960)
XLA Ops:
  19.8 5.6 all-gather.13
  26.0 5.7 all-gather.5
  33.6 12.2 %all-reduce.17 = (bf16[2304]{0:T(1024)(128)(2,1)S(1)}, bf16[384]{0:T(512)(128)(2,1)S(1)}, bf16[384]{0:T(512)(128)(2,1)S(1)}, bf16[2304]{0:T(1024)(128)(2,1)S(1)}...) all-reduce(bf16[2304]{0:T(1024)(128)(2,1)S(1)} %dynamic-update-slice, ...), channel_id=3, replica_groups=mesh['dp'=8,'fsdp'=4] {'fsdp'}, use_global_device_ids=true, to_apply=%add | all-reduce | flops 6144 | bytes 24576
  46.9 8.1 %all-gather.16 = bf16[1,384,384]{2,1,0:T(8,128)(2,1)} all-gather(bf16[1,96,384]{2,1,0:T(8,128)(2,1)S(1)} %get-tuple-element.83), channel_id=18, replica_groups=mesh['dp'=8,'fsdp'=4] {'fsdp'}, dimensions={1}, use_global_device_ids=true | all-gather | bytes 368640 | tf_op jit(solution)/shard_map/all_gather | solution.py:288
  55.1 9.7 %all-gather.10 = bf16[1,384,1152]{2,1,0:T(8,128)(2,1)} all-gather(bf16[1,96,1152]{2,1,0:T(8,128)(2,1)S(1)} %get-tuple-element.81), channel_id=12, replica_groups=mesh['dp'=8,'fsdp'=4] {'fsdp'}, dimensions={1}, use_global_device_ids=true | all-gather | bytes 1105920 | tf_op jit(solution)/shard_map/all_gather | solution.py:262
  64.7 12.8 %all-gather.2 = bf16[1,384,1152]{2,1,0:T(8,128)(2,1)S(1)} all-gather(bf16[1,96,1152]{2,1,0:T(8,128)(2,1)S(1)} %get-tuple-element.82), channel_id=4, replica_groups=mesh['dp'=8,'fsdp'=4] {'fsdp'}, dimensions={1}, use_global_device_ids=true | all-gather | bytes 1105920 | tf_op jit(solution)/shard_map/all_gather | solution.py:262
  77.6 6.5 all-gather.17
  106.8 5.2 fusion.202
  131.1 5.0 fusion.106
  139.3 7.2 fusion.207
  161.0 9.1 %fusion.90 = bf16[3,256,1,6,64]{1,4,3,0,2:T(8,128)(2,1)} fusion(f32[3,6,256,256]{2,3,1,0:T(8,128)} %fusion.157, bf16[3,256,3,6,64]{1,4,3,2,0:T(8,128)(2,1)} %bitcast.265, f32[3,6,256,256]{2,3,1,0:T(8,128)} %copy-done.27, f32[3,6,256]{2,1,0:T(8,128)S(1)} %copy-done.92), kind=kOutput, calls=%fused_computation.109 | convolution fusion | flops 159552256 | bytes 20103168 | tf_op jit(solution)/shard_map/shqk,skhd->sqhd/dot_general | solution.py:35
  170.1 9.1 %fusion.87 = bf16[3,256,1,6,64]{1,4,3,0,2:T(8,128)(2,1)} fusion(f32[3,6,256,256]{2,3,1,0:T(8,128)} %fusion.157, bf16[3,256,3,6,64]{1,4,3,2,0:T(8,128)(2,1)} %bitcast.266, f32[3,6,256,256]{2,3,1,0:T(8,128)} %copy-done.27, f32[3,6,256]{2,1,0:T(8,128)S(1)} %copy-done.92), kind=kOutput, calls=%fused_computation.108 | convolution fusion | flops 159552256 | bytes 20103168 | tf_op jit(solution)/shard_map/shqk,sqhd->skhd/dot_general | solution.py:35
  194.3 4.6 fusion.208
  206.9 4.4 convolution_bitcast_fusion.4
  220.5 9.1 %fusion.96 = bf16[3,256,1,6,64]{1,4,3,0,2:T(8,128)(2,1)} fusion(f32[3,6,256,256]{2,3,1,0:T(8,128)} %fusion.155, bf16[3,256,3,6,64]{1,4,3,2,0:T(8,128)(2,1)} %bitcast.260, f32[3,6,256,256]{2,3,1,0:T(8,128)} %copy-done.26, f32[3,6,256]{2,1,0:T(8,128)} %copy-done.90), kind=kOutput, calls=%fused_computation.111 | convolution fusion | flops 159552256 | bytes 20103168 | tf_op jit(solution)/shard_map/shqk,skhd->sqhd/dot_general | solution.py:35
  229.6 9.0 %fusion.93 = bf16[3,256,1,6,64]{1,4,3,0,2:T(8,128)(2,1)} fusion(f32[3,6,256,256]{2,3,1,0:T(8,128)} %fusion.155, bf16[3,256,3,6,64]{1,4,3,2,0:T(8,128)(2,1)} %bitcast.261, f32[3,6,256,256]{2,3,1,0:T(8,128)} %copy-done.26, f32[3,6,256]{2,1,0:T(8,128)} %copy-done.90), kind=kOutput, calls=%fused_computation.110 | convolution fusion | flops 159552256 | bytes 20103168 | tf_op jit(solution)/shard_map/shqk,sqhd->skhd/dot_general | solution.py:35
  247.3 6.5 convolution_bitcast_fusion
  254.4 4.3 convolution_bitcast_fusion.2
  260.0 6.3 convolution_bitcast_fusion.1
  267.1 4.3 convolution_bitcast_fusion.3
  275.1 4.7 fusion.85
  288.2 4.3 fusion.86
  295.2 35.4 %reduce-scatter.29.cloned.1.call-done = f32[384,384]{1,0:T(8,128)} async-done(((f32[1536,384]{1,0:T(8,128)}), f32[384,384]{1,0:T(8,128)}) %reduce-scatter.29.cloned.1.call-update) | async-done | bytes 589840 | tf_op jit(solution)/shard_map/reduce_scatter | solution.py:306
  330.6 35.2 %reduce-scatter.25.cloned.1.call-done = f32[96,1536]{1,0:T(8,128)} async-done(((f32[384,1536]{1,0:T(8,128)}), f32[96,1536]{1,0:T(8,128)}) %reduce-scatter.25.cloned.1.call-update) | async-done | bytes 589840 | tf_op jit(solution)/shard_map/reduce_scatter | solution.py:304
  365.8 35.4 %reduce-scatter.27.cloned.1.call-done = f32[384,384]{1,0:T(8,128)} async-done(((f32[1536,384]{1,0:T(8,128)}), f32[384,384]{1,0:T(8,128)}) %reduce-scatter.27.cloned.1.call-update) | async-done | bytes 589840 | tf_op jit(solution)/shard_map/reduce_scatter | solution.py:306
  401.2 35.2 %reduce-scatter.23.cloned.1.call-done = f32[96,1536]{1,0:T(8,128)} async-done(((f32[384,1536]{1,0:T(8,128)}), f32[96,1536]{1,0:T(8,128)}) %reduce-scatter.23.cloned.1.call-update) | async-done | bytes 589840 | tf_op jit(solution)/shard_map/reduce_scatter | solution.py:304
  436.4 42.8 %reduce-scatter.13.cloned.1.call-done = f32[96,2304]{1,0:T(8,128)} async-done(((f32[384,2304]{1,0:T(8,128)}), f32[96,2304]{1,0:T(8,128)}) %reduce-scatter.13.cloned.1.call-update) | async-done | bytes 884752 | tf_op jit(solution)/shard_map/reduce_scatter | solution.py:299
  479.2 42.8 %reduce-scatter.11.cloned.1.call-done = f32[96,2304]{1,0:T(8,128)} async-done(((f32[384,2304]{1,0:T(8,128)}), f32[96,2304]{1,0:T(8,128)}) %reduce-scatter.11.cloned.1.call-update) | async-done | bytes 884752 | tf_op jit(solution)/shard_map/reduce_scatter | solution.py:299
  530.6 11.0 %all-reduce.16 = (f32[2304]{0:T(1024)S(1)}, f32[2304]{0:T(1024)S(1)}, f32[384]{0:T(512)S(1)}, f32[384]{0:T(512)S(1)}, f32[1536]{0:T(1024)S(1)}, /*index=5*/f32[1536]{0:T(1024)S(1)}, f32[384]{0:T(512)S(1)}, f32[384]{0:T(512)S(1)}) all-reduce(f32[2304]{0:T(1024)S(1)} %reduce_sum.457, ...), channel_id=23, replica_groups=mesh['dp'=8,'fsdp'=4] {'fsdp'}, use_global_device_ids=true, to_apply=%region_46.47.clone | all-reduce | flops 9216 | bytes 73728
  542.2 40.0 %all-reduce.14 = (f32[1,576]{1,0:T(1,128)S(1)}, f32[1,576]{1,0:T(1,128)S(1)}, f32[1,96]{1,0:T(1,128)S(1)}, f32[1,96]{1,0:T(1,128)S(1)}, f32[1,384]{1,0:T(1,128)S...) all-reduce(f32[1,576]{1,0:T(1,128)S(1)} %stack.125, ...), channel_id=1, replica_groups=mesh['dp'=8,'fsdp'=4] {'dp'}, use_global_device_ids=true, to_apply=%region_47.48 | all-reduce | flops 2304 | bytes 18432 | tf_op jit(solution)/shard_map/psum | solution.py:309
  590.6 5.0 fusion.70
  595.6 117.3 %all-reduce.20.cloned.1.call-done = (f32[1,96,2304]{2,1,0:T(8,128)}, f32[1,96,2304]{2,1,0:T(8,128)}, f32[1,96,1152]{2,1,0:T(8,128)}, f32[1,96,1152]{2,1,0:T(8,12...) async-done(((f32[1,96,2304]{2,1,0:T(8,128)}, ...) | async-done | bytes 5308432 | tf_op jit(solution)/shard_map/psum | solution.py:309
  (474 shorter events, 153.3 us)
Async XLA Ops:
  7.2 80.7 %all-gather.25.cloned.1.call-start = ((), (), s32[]{:S(2)}) async-start(), calls=%async_computation.20 | async-start | bytes 2211840 | tf_op jit(solution)/shard_map/all_gather | solution.py:260
  9.5 80.9 %all-gather.31.cloned.1.call-start = ((), (), s32[]{:S(2)}) async-start(), calls=%async_computation.23 | async-start | bytes 2211840 | tf_op jit(solution)/shard_map/all_gather | solution.py:260
  10.2 96.6 %all-gather.27.cloned.1.call-start = ((), (), s32[]{:S(2)}) async-start(), calls=%async_computation.21 | async-start | bytes 1474560 | tf_op jit(solution)/shard_map/all_gather | solution.py:265
  11.2 95.6 %all-gather.29.cloned.1.call-start = ((), (), s32[]{:S(2)}) async-start(), calls=%async_computation.22 | async-start | bytes 1474560 | tf_op jit(solution)/shard_map/all_gather | solution.py:267
  12.1 119.0 %all-gather.33.cloned.1.call-start = ((), (), s32[]{:S(2)}) async-start(), calls=%async_computation.24 | async-start | bytes 1474560 | tf_op jit(solution)/shard_map/all_gather | solution.py:265
  12.7 126.6 %all-gather.35.cloned.1.call-start = ((), (), s32[]{:S(2)}) async-start(), calls=%async_computation.25 | async-start | bytes 1474560 | tf_op jit(solution)/shard_map/all_gather | solution.py:267
  13.4 41.6 %copy-start.55 = (bf16[2,96,1152]{2,1,0:T(8,128)(2,1)S(1)}, bf16[2,96,1152]{2,1,0:T(8,128)(2,1)}, u32[]{:S(2)}) copy-start(bf16[2,96,1152]{2,1,0:T(8,128)(2,1)} %param.19) | copy-start | bytes 1327108
  13.4 70.7 %collective-permute-start = (bf16[96,384]{1,0:T(8,128)(2,1)S(1)}, bf16[96,384]{1,0:T(8,128)(2,1)S(1)}, u32[]{:S(2)}, u32[]{:S(2)}) collective-permute-start(bf16[96,384]{1,0:T(8,128)(2,1)S(1)} %get-tuple-element.84), channel_id=1, source_target_pairs={{0,1},{1,2},{2,3},{3,0},{4,5},{5,6},{6,7},{7,4},{8,9},{9,10},{10,1... | collective-permute-start | bytes 221192 | tf_op jit(solution)/shard_map/ppermute | solution.py:22
  13.9 70.5 %collective-permute-start.1 = (bf16[96,384]{1,0:T(8,128)(2,1)S(1)}, bf16[96,384]{1,0:T(8,128)(2,1)S(1)}, u32[]{:S(2)}, u32[]{:S(2)}) collective-permute-start(bf16[96,384]{1,0:T(8,128)(2,1)S(1)} %get-tuple-element.84), channel_id=1, source_target_pairs={{0,3},{1,0},{2,1},{3,2},{4,7},{5,4},{6,5},{7,6},{8,11},{9,8},{10,9... | collective-permute-start | bytes 221192 | tf_op jit(solution)/shard_map/ppermute | solution.py:27
  15.9 279.1 %reduce-scatter.21.cloned.1.call-start = ((), (), s32[]{:S(2)}) async-start(), calls=%async_computation.15 | async-start | bytes 737280 | tf_op jit(solution)/shard_map/reduce_scatter | solution.py:302
  19.4 73.6 %copy-start.75 = (f32[3,256]{1,0:T(4,128)}, f32[3,256]{1,0:T(4,128)S(1)}, u32[]{:S(2)}) copy-start(f32[3,256]{1,0:T(4,128)S(1)} %broadcast_multiply_fusion.13) | copy-start | bytes 9220
  19.8 73.3 %copy-start.100 = (f32[3,256]{1,0:T(4,128)}, f32[3,256]{1,0:T(4,128)S(1)}, u32[]{:S(2)}) copy-start(f32[3,256]{1,0:T(4,128)S(1)} %add_rsqrt_fusion.5) | copy-start | bytes 9220
  45.8 59.3 %copy-start.98 = (f32[384]{0:T(512)}, f32[384]{0:T(512)S(1)}, u32[]{:S(2)}) copy-start(f32[384]{0:T(512)S(1)} %convert_element_type.206) | copy-start | bytes 4612
  84.1 3.8 collective-permute-start.2
  93.0 36.0 %copy-start.60 = (f32[3,384]{1,0:T(4,128)}, f32[3,384]{1,0:T(4,128)S(1)}, u32[]{:S(2)}) copy-start(f32[3,384]{1,0:T(4,128)S(1)} %get-tuple-element.92) | copy-start | bytes 13828
  184.9 110.1 %reduce-scatter.19.cloned.1.call-start = ((), (), s32[]{:S(2)}) async-start(), calls=%async_computation.14 | async-start | bytes 737280 | tf_op jit(solution)/shard_map/reduce_scatter | solution.py:302
  206.9 88.2 %reduce-scatter.17.cloned.1.call-start = ((), (), s32[]{:S(2)}) async-start(), calls=%async_computation.13 | async-start | bytes 2211840 | tf_op jit(solution)/shard_map/reduce_scatter | solution.py:301
  211.3 83.9 %reduce-scatter.15.cloned.1.call-start = ((), (), s32[]{:S(2)}) async-start(), calls=%async_computation.12 | async-start | bytes 2211840 | tf_op jit(solution)/shard_map/reduce_scatter | solution.py:301
  246.6 84.0 %reduce-scatter.29.cloned.1.call-start = ((), (), s32[]{:S(2)}) async-start(), calls=%async_computation.19 | async-start | bytes 2949120 | tf_op jit(solution)/shard_map/reduce_scatter | solution.py:306
  253.8 112.0 %reduce-scatter.25.cloned.1.call-start = ((), (), s32[]{:S(2)}) async-start(), calls=%async_computation.17 | async-start | bytes 2949120 | tf_op jit(solution)/shard_map/reduce_scatter | solution.py:304
  258.8 142.4 %reduce-scatter.27.cloned.1.call-start = ((), (), s32[]{:S(2)}) async-start(), calls=%async_computation.18 | async-start | bytes 2949120 | tf_op jit(solution)/shard_map/reduce_scatter | solution.py:306
  266.4 170.0 %reduce-scatter.23.cloned.1.call-start = ((), (), s32[]{:S(2)}) async-start(), calls=%async_computation.16 | async-start | bytes 2949120 | tf_op jit(solution)/shard_map/reduce_scatter | solution.py:304
  271.4 207.8 %reduce-scatter.13.cloned.1.call-start = ((), (), s32[]{:S(2)}) async-start(), calls=%async_computation.11 | async-start | bytes 4423680 | tf_op jit(solution)/shard_map/reduce_scatter | solution.py:299
  282.9 239.1 %reduce-scatter.11.cloned.1.call-start = ((), (), s32[]{:S(2)}) async-start(), calls=%async_computation.10 | async-start | bytes 4423680 | tf_op jit(solution)/shard_map/reduce_scatter | solution.py:299
  295.0 418.0 %all-reduce.20.cloned.1.call-start = ((), (), s32[]{:S(2)}) async-start(), calls=%async_computation.26 | async-start | bytes 10616832 | tf_op jit(solution)/shard_map/psum | solution.py:309
  522.1 62.5 %copy-start.13 = (bf16[3,6,64,256]{3,2,1,0:T(8,128)(2,1)S(1)}, bf16[3,6,64,256]{3,2,1,0:T(8,128)(2,1)}, u32[]{:S(2)}) copy-start(bf16[3,6,64,256]{3,2,1,0:T(8,128)(2,1)} %copy-done.11) | copy-start | bytes 1769476
  522.1 62.5 %copy-start.62 = (f32[3,384]{1,0:T(4,128)S(1)}, f32[3,384]{1,0:T(4,128)}, u32[]{:S(2)}) copy-start(f32[3,384]{1,0:T(4,128)} %copy-done.60) | copy-start | bytes 13828
  522.1 62.5 %copy-start.97 = (f32[384]{0:T(512)S(1)}, f32[384]{0:T(512)}, u32[]{:S(2)}) copy-start(f32[384]{0:T(512)} %convert_element_type.209) | copy-start | bytes 4612
  522.1 62.5 %copy-start.3 = (f32[3,256,384]{2,1,0:T(8,128)S(1)}, f32[3,256,384]{2,1,0:T(8,128)}, u32[]{:S(2)}) copy-start(f32[3,256,384]{2,1,0:T(8,128)} %copy-done.1) | copy-start | bytes 3538948
  522.2 4.3 collective-permute-start.3
  522.2 5.1 collective-permute-start.4
  526.5 4.0 collective-permute-start.5
  (123 other events, 465.9 us)
Sparse Core Ops, SparseCore 0:
  10.1 23.5 all-gather.24
  35.9 22.2 all-gather.30
  60.4 20.4 all-gather.26
  82.9 18.0 all-gather.28
  102.4 17.4 all-gather.32
  121.9 17.4 all-gather.34
  185.1 22.0 reduce-scatter.20
  209.7 22.0 reduce-scatter.18
  234.3 29.1 reduce-scatter.16
  266.0 29.1 reduce-scatter.14
  297.7 32.8 reduce-scatter.28
  333.0 32.8 reduce-scatter.24
  368.4 32.8 reduce-scatter.26
  403.6 32.8 reduce-scatter.22
  438.9 40.3 reduce-scatter.12
  481.7 40.3 reduce-scatter.10
  526.7 186.2 all-reduce.19
